TPU v7x, 128 devices: a whole 4x4x4 slice. The times are simulated.
128 devices in a mesh: leaf: 8 (over x, core), prow: 4 (over z), pcol: 4 (over y).
Axes of the slice: x: 4, y: 4, z: 4, core: 2. Of those that a mesh axis runs over, the one named last changes fastest.
Arguments:
- subtree_factor: float32 [8, 2, 8, 256, 2048], P('leaf', None, None, 'prow', 'pcol'), may hold values from -0.09375 to 0.09375
- sub_linv: float32 [8, 2, 8, 256, 256], P('leaf', None, None, 'prow'), may hold values from -0.05 to 1.05
- sub_uinv: float32 [8, 2, 8, 256, 256], P('leaf', None, None, 'prow'), may hold values from -0.05 to 1.05
- lower_panel: float32 [8, 4, 256, 2, 2048], P('leaf', None, 'prow', None, 'pcol'), may hold values from -0.0234375 to 0.0234375
- upper_panel: float32 [8, 2, 8, 256, 1024], P('leaf', None, None, 'prow', 'pcol'), may hold values from -0.125 to 0.125
- panel_rows: int32 [8, 4, 2], P('leaf'), may hold values 0 or 1
- upper_level_factor: float32 [4, 256, 1024], P(None, 'prow', 'pcol'), may hold values from -0.125 to 0.125
- top_linv: float32 [4, 256, 256], P(None, 'prow'), may hold values from -0.05 to 1.05
- top_uinv: float32 [4, 256, 256], P(None, 'prow'), may hold values from -0.05 to 1.05
- sub_rhs: float32 [8, 2, 8, 256, 256], P('leaf', None, None, 'prow'), may hold values from -6 to 6
- top_rhs: float32 [4, 256, 256], P(None, 'prow', 'leaf'), may hold values from -6 to 6
Outputs:
- sub_solution: float32 [8, 2, 8, 256, 256], P('leaf', None, 'pcol')
- top_solution: float32 [4, 256, 256], P('pcol', None, 'leaf')
All inputs are finite; a program needn't handle non-finite values. No bound on the sum of `panel_rows` on one device may be relied on, other than what follows from the above.
Results may differ from a plain program's by a relative error of at most 0.00013.
Values sent between devices are 32-bit elements; how exact they have to be, the bound alone decides.
A program may use at most 128 MiB of HBM per device.

v0:
```python
import jax
import jax.numpy as jnp
from jax import lax
from jax.sharding import PartitionSpec as P

TOP_PRECISION = lax.Precision.HIGHEST


def block_order(block_count, forward):
    return range(block_count) if forward else range(block_count - 1, -1, -1)


def sweep_blocks(factor_row_block, inverses, right_side, coupling, owned_start, my_col, forward):
    groups, block_count, tile_rows, columns = right_side.shape
    block_rows = inverses.shape[3]
    owned_count = factor_row_block.shape[3] // block_rows
    solved = jnp.zeros((groups, block_count, block_rows, columns), jnp.float32)
    for sweep_step_index in block_order(block_count, forward):
        held_value_entries = lax.dynamic_slice_in_dim(solved, owned_start, owned_count, 1)
        held_value_entries = held_value_entries.reshape(groups, owned_count * block_rows, columns)
        partial_value = coupling[:, sweep_step_index] + jnp.einsum(
            "pht,ptj->phj",
            factor_row_block[:, sweep_step_index],
            held_value_entries,
            precision=TOP_PRECISION,
        )
        local_side = jnp.where(my_col == 0, right_side[:, sweep_step_index], 0.0) - partial_value
        inverse_part = jnp.einsum(
            "gab,gar->gbr", inverses[:, sweep_step_index], local_side, precision=TOP_PRECISION
        )
        block_value = lax.psum(inverse_part, ("prow", "pcol"))
        solved = solved.at[:, sweep_step_index].set(block_value)
    return solved


def per_device(
    subtree_factor,
    sub_linv,
    sub_uinv,
    lower_panel,
    upper_panel,
    panel_rows,
    upper_level_factor,
    top_linv,
    top_uinv,
    sub_rhs,
    top_rhs,
):
    my_row = lax.axis_index("prow")
    my_col = lax.axis_index("pcol")
    block_rows = sub_linv.shape[4]
    tile_rows = sub_rhs.shape[3]
    groups = sub_rhs.shape[1]
    block_count = sub_rhs.shape[2]
    sub_owned = subtree_factor.shape[4] // block_rows
    top_owned = upper_level_factor.shape[2] // block_rows
    present = panel_rows[0].astype(jnp.float32)
    linv_rows, uinv_rows, top_linv_rows, top_uinv_rows = (sub_linv, sub_uinv, top_linv, top_uinv)
    lower_sub = sweep_blocks(
        subtree_factor[0],
        linv_rows[0],
        sub_rhs[0],
        jnp.zeros(sub_rhs[0].shape, jnp.float32),
        my_col * sub_owned,
        my_col,
        True,
    )
    lower_owned = lax.dynamic_slice_in_dim(lower_sub, my_col * sub_owned, sub_owned, 1)
    lower_owned = lower_owned.reshape(groups, sub_owned * block_rows, lower_sub.shape[3])
    contrib_part = jnp.einsum(
        "tasm,ts,smr->tar", lower_panel[0], present, lower_owned, precision=TOP_PRECISION
    )
    contrib = lax.psum(contrib_part, "leaf")
    upper_level_side = lax.all_gather(top_rhs, "leaf", axis=2, tiled=True)
    upper_level_lower = sweep_blocks(
        upper_level_factor[None],
        top_linv_rows[None],
        upper_level_side[None],
        contrib[None],
        my_col * top_owned,
        my_col,
        True,
    )
    top_rows = lax.dynamic_slice_in_dim(upper_level_lower, my_row * tile_rows, tile_rows, 2)
    top_upper = sweep_blocks(
        upper_level_factor[None],
        top_uinv_rows[None],
        top_rows,
        jnp.zeros(top_rows.shape, jnp.float32),
        my_col * top_owned,
        my_col,
        False,
    )[0]
    top_out = lax.dynamic_slice_in_dim(
        top_upper, lax.axis_index("leaf") * top_rhs.shape[2], top_rhs.shape[2], 2
    )
    top_out = lax.dynamic_slice_in_dim(top_out, my_col * top_owned, top_owned, 0)
    top_mine = lax.dynamic_slice_in_dim(top_upper, my_col * top_owned, top_owned, 0)
    mask_mine = lax.dynamic_slice_in_dim(present, my_col * top_owned, top_owned, 0)
    upper_local = upper_panel[0].reshape(groups, block_count, tile_rows, top_owned, block_rows)
    coupling = jnp.einsum(
        "skatb,ts,tbr->skar", upper_local, mask_mine, top_mine, precision=TOP_PRECISION
    )
    sub_rows = lax.dynamic_slice_in_dim(lower_sub, my_row * tile_rows, tile_rows, 2)
    upper_sub = sweep_blocks(
        subtree_factor[0], uinv_rows[0], sub_rows, coupling, my_col * sub_owned, my_col, False
    )
    sub_out = lax.dynamic_slice_in_dim(upper_sub, my_col * sub_owned, sub_owned, 1)
    return (sub_out[None], top_out)


def solution(mesh):
    placed = (
        P("leaf", None, None, "prow", "pcol"),
        P("leaf", None, None, "prow", None),
        P("leaf", None, None, "prow", None),
        P("leaf", None, "prow", None, "pcol"),
        P("leaf", None, None, "prow", "pcol"),
        P("leaf", None, None),
        P(None, "prow", "pcol"),
        P(None, "prow", None),
        P(None, "prow", None),
        P("leaf", None, None, "prow", None),
        P(None, "prow", "leaf"),
    )
    return jax.shard_map(
        per_device,
        mesh=mesh,
        in_specs=placed,
        out_specs=(P("leaf", None, "pcol", None, None), P("pcol", None, "leaf")),
        check_vma=False,
    )
```

profile of v0, /device:TPU:0, one launch (start us, length us, event | category | flops | bytes accessed | tf_op | source)
XLA Modules:
  0.0 2303.5 jit_solution(17855429060302195027)
XLA Ops:
  15.9 88.4 %all-reduce.30.cloned.1.call-done = f32[2,1,256,256]{3,2,0,1:T(8,128)} async-done(((f32[2,1,256,256]{3,2,0,1:T(8,128)}), f32[2,1,256,256]{3,2,0,1:T(8,128)}) %all-reduce.30.cloned.1.call-update) | async-done | bytes 524304 | tf_op jit(solution)/shard_map/psum | solution.py:31
  113.0 80.7 %all-reduce.32.cloned.1.call-done = f32[2,1,256,256]{3,2,0,1:T(8,128)} async-done(((f32[2,1,256,256]{3,2,0,1:T(8,128)}), f32[2,1,256,256]{3,2,0,1:T(8,128)}) %all-reduce.32.cloned.1.call-update) | async-done | bytes 524304 | tf_op jit(solution)/shard_map/psum | solution.py:31
  201.2 85.3 %all-reduce.34.cloned.1.call-done = f32[2,1,256,256]{3,2,0,1:T(8,128)} async-done(((f32[2,1,256,256]{3,2,0,1:T(8,128)}), f32[2,1,256,256]{3,2,0,1:T(8,128)}) %all-reduce.34.cloned.1.call-update) | async-done | bytes 524304 | tf_op jit(solution)/shard_map/psum | solution.py:31
  293.9 85.3 %all-reduce.36.cloned.1.call-done = f32[2,1,256,256]{3,2,0,1:T(8,128)} async-done(((f32[2,1,256,256]{3,2,0,1:T(8,128)}), f32[2,1,256,256]{3,2,0,1:T(8,128)}) %all-reduce.36.cloned.1.call-update) | async-done | bytes 524304 | tf_op jit(solution)/shard_map/psum | solution.py:31
  386.6 85.3 %all-reduce.38.cloned.1.call-done = f32[2,1,256,256]{3,2,0,1:T(8,128)} async-done(((f32[2,1,256,256]{3,2,0,1:T(8,128)}), f32[2,1,256,256]{3,2,0,1:T(8,128)}) %all-reduce.38.cloned.1.call-update) | async-done | bytes 524304 | tf_op jit(solution)/shard_map/psum | solution.py:31
  479.3 85.2 %all-reduce.40.cloned.1.call-done = f32[2,1,256,256]{3,2,0,1:T(8,128)} async-done(((f32[2,1,256,256]{3,2,0,1:T(8,128)}), f32[2,1,256,256]{3,2,0,1:T(8,128)}) %all-reduce.40.cloned.1.call-update) | async-done | bytes 524304 | tf_op jit(solution)/shard_map/psum | solution.py:31
  572.0 85.3 %all-reduce.42.cloned.1.call-done = f32[2,1,256,256]{3,2,0,1:T(8,128)} async-done(((f32[2,1,256,256]{3,2,0,1:T(8,128)}), f32[2,1,256,256]{3,2,0,1:T(8,128)}) %all-reduce.42.cloned.1.call-update) | async-done | bytes 524304 | tf_op jit(solution)/shard_map/psum | solution.py:31
  667.6 82.2 %all-reduce.44.cloned.1.call-done = f32[2,1,256,256]{3,2,0,1:T(8,128)} async-done(((f32[2,1,256,256]{3,2,0,1:T(8,128)}), f32[2,1,256,256]{3,2,0,1:T(8,128)}) %all-reduce.44.cloned.1.call-update) | async-done | bytes 524304 | tf_op jit(solution)/shard_map/psum | solution.py:31
  816.8 85.7 %all-reduce.48.cloned.1.call-done = f32[1,1,256,256]{3,2,1,0:T(8,128)} async-done(((f32[1,1,256,256]{3,2,1,0:T(8,128)}), f32[1,1,256,256]{3,2,1,0:T(8,128)}) %all-reduce.48.cloned.1.call-update) | async-done | bytes 262160 | tf_op jit(solution)/shard_map/psum | solution.py:31
  907.9 82.4 %all-reduce.50.cloned.1.call-done = f32[1,1,256,256]{3,2,1,0:T(8,128)} async-done(((f32[1,1,256,256]{3,2,1,0:T(8,128)}), f32[1,1,256,256]{3,2,1,0:T(8,128)}) %all-reduce.50.cloned.1.call-update) | async-done | bytes 262160 | tf_op jit(solution)/shard_map/psum | solution.py:31
  995.2 84.5 %all-reduce.52.cloned.1.call-done = f32[1,1,256,256]{3,2,1,0:T(8,128)} async-done(((f32[1,1,256,256]{3,2,1,0:T(8,128)}), f32[1,1,256,256]{3,2,1,0:T(8,128)}) %all-reduce.52.cloned.1.call-update) | async-done | bytes 262160 | tf_op jit(solution)/shard_map/psum | solution.py:31
  1084.7 84.5 %all-reduce.54.cloned.1.call-done = f32[1,1,256,256]{3,2,1,0:T(8,128)} async-done(((f32[1,1,256,256]{3,2,1,0:T(8,128)}), f32[1,1,256,256]{3,2,1,0:T(8,128)}) %all-reduce.54.cloned.1.call-update) | async-done | bytes 262160 | tf_op jit(solution)/shard_map/psum | solution.py:31
  1173.0 84.5 %all-reduce.56.cloned.1.call-done = f32[1,1,256,256]{2,3,1,0:T(8,128)} async-done(((f32[1,1,256,256]{2,3,1,0:T(8,128)}), f32[1,1,256,256]{2,3,1,0:T(8,128)}) %all-reduce.56.cloned.1.call-update) | async-done | bytes 262160 | tf_op jit(solution)/shard_map/psum | solution.py:31
  1262.8 82.5 %all-reduce.58.cloned.1.call-done = f32[1,1,256,256]{2,3,1,0:T(8,128)} async-done(((f32[1,1,256,256]{2,3,1,0:T(8,128)}), f32[1,1,256,256]{2,3,1,0:T(8,128)}) %all-reduce.58.cloned.1.call-update) | async-done | bytes 262160 | tf_op jit(solution)/shard_map/psum | solution.py:31
  1350.3 84.5 %all-reduce.60.cloned.1.call-done = f32[1,1,256,256]{2,3,1,0:T(8,128)} async-done(((f32[1,1,256,256]{2,3,1,0:T(8,128)}), f32[1,1,256,256]{2,3,1,0:T(8,128)}) %all-reduce.60.cloned.1.call-update) | async-done | bytes 262160 | tf_op jit(solution)/shard_map/psum | solution.py:31
  1442.3 82.0 %all-reduce.62.cloned.1.call-done = f32[1,256,256]{1,2,0:T(8,128)} async-done(((f32[1,256,256]{1,2,0:T(8,128)}), f32[1,256,256]{1,2,0:T(8,128)}) %all-reduce.62.cloned.1.call-update) | async-done | bytes 262160 | tf_op jit(solution)/shard_map/psum | solution.py:31
  1534.6 85.1 %all-reduce.64.cloned.1.call-done = f32[2,1,256,256]{2,3,0,1:T(8,128)} async-done(((f32[2,1,256,256]{2,3,0,1:T(8,128)}), f32[2,1,256,256]{2,3,0,1:T(8,128)}) %all-reduce.64.cloned.1.call-update) | async-done | bytes 524304 | tf_op jit(solution)/shard_map/psum | solution.py:31
  1632.5 81.6 %all-reduce.66.cloned.1.call-done = f32[2,1,256,256]{2,3,0,1:T(8,128)} async-done(((f32[2,1,256,256]{2,3,0,1:T(8,128)}), f32[2,1,256,256]{2,3,0,1:T(8,128)}) %all-reduce.66.cloned.1.call-update) | async-done | bytes 524304 | tf_op jit(solution)/shard_map/psum | solution.py:31
  1725.3 85.2 %all-reduce.68.cloned.1.call-done = f32[2,1,256,256]{2,3,0,1:T(8,128)} async-done(((f32[2,1,256,256]{2,3,0,1:T(8,128)}), f32[2,1,256,256]{2,3,0,1:T(8,128)}) %all-reduce.68.cloned.1.call-update) | async-done | bytes 524304 | tf_op jit(solution)/shard_map/psum | solution.py:31
  1821.7 85.2 %all-reduce.70.cloned.1.call-done = f32[2,1,256,256]{2,3,0,1:T(8,128)} async-done(((f32[2,1,256,256]{2,3,0,1:T(8,128)}), f32[2,1,256,256]{2,3,0,1:T(8,128)}) %all-reduce.70.cloned.1.call-update) | async-done | bytes 524304 | tf_op jit(solution)/shard_map/psum | solution.py:31
  1918.0 85.2 %all-reduce.72.cloned.1.call-done = f32[2,1,256,256]{2,3,0,1:T(8,128)} async-done(((f32[2,1,256,256]{2,3,0,1:T(8,128)}), f32[2,1,256,256]{2,3,0,1:T(8,128)}) %all-reduce.72.cloned.1.call-update) | async-done | bytes 524304 | tf_op jit(solution)/shard_map/psum | solution.py:31
  2014.4 85.3 %all-reduce.74.cloned.1.call-done = f32[2,1,256,256]{2,3,0,1:T(8,128)} async-done(((f32[2,1,256,256]{2,3,0,1:T(8,128)}), f32[2,1,256,256]{2,3,0,1:T(8,128)}) %all-reduce.74.cloned.1.call-update) | async-done | bytes 524304 | tf_op jit(solution)/shard_map/psum | solution.py:31
  2110.9 85.2 %all-reduce.76.cloned.1.call-done = f32[2,1,256,256]{2,3,0,1:T(8,128)} async-done(((f32[2,1,256,256]{2,3,0,1:T(8,128)}), f32[2,1,256,256]{2,3,0,1:T(8,128)}) %all-reduce.76.cloned.1.call-update) | async-done | bytes 524304 | tf_op jit(solution)/shard_map/psum | solution.py:31
  2208.7 83.8 %all-reduce.78.cloned.1.call-done = f32[2,1,256,256]{2,3,0,1:T(8,128)} async-done(((f32[2,1,256,256]{2,3,0,1:T(8,128)}), f32[2,1,256,256]{2,3,0,1:T(8,128)}) %all-reduce.78.cloned.1.call-update) | async-done | bytes 524304 | tf_op jit(solution)/shard_map/psum | solution.py:31
  (184 shorter events, 264.3 us)
Async XLA Ops:
  15.8 177.9 %all-reduce.32.cloned.1.call-start = ((), (), s32[]{:S(2)}) async-start(), calls=%async_computation.1 | async-start | bytes 1048576 | tf_op jit(solution)/shard_map/psum | solution.py:31
  109.6 176.9 %all-reduce.34.cloned.1.call-start = ((), (), s32[]{:S(2)}) async-start(), calls=%async_computation.2 | async-start | bytes 1048576 | tf_op jit(solution)/shard_map/psum | solution.py:31
  201.1 178.0 %all-reduce.36.cloned.1.call-start = ((), (), s32[]{:S(2)}) async-start(), calls=%async_computation.3 | async-start | bytes 1048576 | tf_op jit(solution)/shard_map/psum | solution.py:31
  293.9 178.0 %all-reduce.38.cloned.1.call-start = ((), (), s32[]{:S(2)}) async-start(), calls=%async_computation.4 | async-start | bytes 1048576 | tf_op jit(solution)/shard_map/psum | solution.py:31
  386.6 177.9 %all-reduce.40.cloned.1.call-start = ((), (), s32[]{:S(2)}) async-start(), calls=%async_computation.5 | async-start | bytes 1048576 | tf_op jit(solution)/shard_map/psum | solution.py:31
  479.3 177.9 %all-reduce.42.cloned.1.call-start = ((), (), s32[]{:S(2)}) async-start(), calls=%async_computation.6 | async-start | bytes 1048576 | tf_op jit(solution)/shard_map/psum | solution.py:31
  571.9 177.9 %all-reduce.44.cloned.1.call-start = ((), (), s32[]{:S(2)}) async-start(), calls=%async_computation.7 | async-start | bytes 1048576 | tf_op jit(solution)/shard_map/psum | solution.py:31
  664.6 150.2 %all-reduce.46.cloned.1.call-start = ((), (), s32[]{:S(2)}) async-start(), calls=%async_computation.8 | async-start | bytes 524288 | tf_op jit(solution)/shard_map/psum | solution.py:73
  755.0 147.5 %all-reduce.48.cloned.1.call-start = ((), (), s32[]{:S(2)}) async-start(), calls=%async_computation.9 | async-start | bytes 524288 | tf_op jit(solution)/shard_map/psum | solution.py:31
  816.8 173.4 %all-reduce.50.cloned.1.call-start = ((), (), s32[]{:S(2)}) async-start(), calls=%async_computation.10 | async-start | bytes 524288 | tf_op jit(solution)/shard_map/psum | solution.py:31
  905.8 173.9 %all-reduce.52.cloned.1.call-start = ((), (), s32[]{:S(2)}) async-start(), calls=%async_computation.11 | async-start | bytes 524288 | tf_op jit(solution)/shard_map/psum | solution.py:31
  995.1 174.0 %all-reduce.54.cloned.1.call-start = ((), (), s32[]{:S(2)}) async-start(), calls=%async_computation.12 | async-start | bytes 524288 | tf_op jit(solution)/shard_map/psum | solution.py:31
  1084.7 172.8 %all-reduce.56.cloned.1.call-start = ((), (), s32[]{:S(2)}) async-start(), calls=%async_computation.13 | async-start | bytes 524288 | tf_op jit(solution)/shard_map/psum | solution.py:31
  1172.9 172.3 %all-reduce.58.cloned.1.call-start = ((), (), s32[]{:S(2)}) async-start(), calls=%async_computation.14 | async-start | bytes 524288 | tf_op jit(solution)/shard_map/psum | solution.py:31
  1260.7 174.1 %all-reduce.60.cloned.1.call-start = ((), (), s32[]{:S(2)}) async-start(), calls=%async_computation.15 | async-start | bytes 524288 | tf_op jit(solution)/shard_map/psum | solution.py:31
  1350.2 174.0 %all-reduce.62.cloned.1.call-start = ((), (), s32[]{:S(2)}) async-start(), calls=%async_computation.16 | async-start | bytes 524288 | tf_op jit(solution)/shard_map/psum | solution.py:31
  1439.8 180.0 %all-reduce.64.cloned.1.call-start = ((), (), s32[]{:S(2)}) async-start(), calls=%async_computation.17 | async-start | bytes 1048576 | tf_op jit(solution)/shard_map/psum | solution.py:31
  1534.6 179.5 %all-reduce.66.cloned.1.call-start = ((), (), s32[]{:S(2)}) async-start(), calls=%async_computation.18 | async-start | bytes 1048576 | tf_op jit(solution)/shard_map/psum | solution.py:31
  1628.9 181.6 %all-reduce.68.cloned.1.call-start = ((), (), s32[]{:S(2)}) async-start(), calls=%async_computation.19 | async-start | bytes 1048576 | tf_op jit(solution)/shard_map/psum | solution.py:31
  1725.2 181.6 %all-reduce.70.cloned.1.call-start = ((), (), s32[]{:S(2)}) async-start(), calls=%async_computation.20 | async-start | bytes 1048576 | tf_op jit(solution)/shard_map/psum | solution.py:31
  1821.6 181.6 %all-reduce.72.cloned.1.call-start = ((), (), s32[]{:S(2)}) async-start(), calls=%async_computation.21 | async-start | bytes 1048576 | tf_op jit(solution)/shard_map/psum | solution.py:31
  1918.0 181.7 %all-reduce.74.cloned.1.call-start = ((), (), s32[]{:S(2)}) async-start(), calls=%async_computation.22 | async-start | bytes 1048576 | tf_op jit(solution)/shard_map/psum | solution.py:31
  2014.3 181.7 %all-reduce.76.cloned.1.call-start = ((), (), s32[]{:S(2)}) async-start(), calls=%async_computation.23 | async-start | bytes 1048576 | tf_op jit(solution)/shard_map/psum | solution.py:31
  2110.8 181.7 %all-reduce.78.cloned.1.call-start = ((), (), s32[]{:S(2)}) async-start(), calls=%async_computation.24 | async-start | bytes 1048576 | tf_op jit(solution)/shard_map/psum | solution.py:31
  (8 other events, 2078.1 us)
Sparse Core Ops, SparseCore 0:
  15.9 88.3 all-reduce.29
  109.7 84.0 all-reduce.31
  201.3 85.1 all-reduce.33
  294.0 85.1 all-reduce.35
  386.7 85.1 all-reduce.37
  479.4 85.0 all-reduce.39
  572.0 85.1 all-reduce.41
  664.7 85.0 all-reduce.43
  818.3 84.1 all-reduce.47
  905.9 84.2 all-reduce.49
  995.3 84.3 all-reduce.51
  1084.8 84.3 all-reduce.53
  1173.1 84.3 all-reduce.55
  1260.8 84.3 all-reduce.57
  1350.4 84.3 all-reduce.59
  1439.9 84.3 all-reduce.61
  1534.7 85.0 all-reduce.63
  1629.0 85.0 all-reduce.65
  1725.3 85.0 all-reduce.67
  1821.7 85.0 all-reduce.69
  1918.1 85.0 all-reduce.71
  2014.5 85.1 all-reduce.73
  2110.9 85.0 all-reduce.75
  2207.4 85.0 all-reduce.77
  (1 shorter events, 59.5 us)
where the time goes:
time: 2310 us; the launch traced here: 2300 us
  waiting for transfers between devices  2070 us (90%)
  local copies, waits for them, and re-layouts  108 us (5%)
  matrix products  93 us (4%)
    psum x24, waiting for transfers between devices, sweep_blocks(): block_value = lax.psum(inverse_part, ('prow', 'pcol'))  2020 us
    dot_general x24, matrix products, sweep_blocks(): jnp.einsum('gab,gar->gbr', inverses[:, sweep_step_index], local_side, pre...  53.3 us
    scatter x24, local copies, waits for them, and re-layouts, sweep_blocks(): solved = solved.at[:, sweep_step_index].set(block_value)  47.2 us
  transfers between devices with their start and end apart: 25, of which 25 were waited for; matrix products, arithmetic and copies ran while one was open for 1% of the time, Pallas kernels for 0%

commit v1 on v0

--- a/solution.py
+++ b/solution.py
@@ -28,7 +28,7 @@
         inverse_part = jnp.einsum(
             "gab,gar->gbr", inverses[:, sweep_step_index], local_side, precision=TOP_PRECISION
         )
-        block_value = lax.psum(inverse_part, ("prow", "pcol"))
+        block_value = jnp.sum(lax.all_gather(inverse_part, ("prow", "pcol")), axis=0)
         solved = solved.at[:, sweep_step_index].set(block_value)
     return solved
 

time: 2310 us -> 2020 us (0.87)
  waiting for transfers between devices: 2070 us -> 1610 us
  other arithmetic: 3.61 us -> 88.3 us
  local copies, waits for them, and re-layouts: 108 us -> 184 us
    psum x24 -> x0, waiting for transfers between devices: 2020 us -> none  [sweep_blocks(): block_value = lax.psum(inverse_part, ('prow', 'pcol'))]
    all_gather x0 -> x24, waiting for transfers between devices: none -> 1560 us  [sweep_blocks(): lax.all_gather(inverse_part, ('prow', 'pcol'))]
    reduce_sum x0 -> x24, other arithmetic: none -> 84.6 us  [sweep_blocks(): jnp.sum(lax.all_gather(inverse_part, ('prow', 'pcol')), axis=0)]
    unnamed x19 -> x37, local copies, waits for them, and re-layouts: 8.4 us -> 54.1 us
    dot_general x0 -> x16, local copies, waits for them, and re-layouts: none -> 31.7 us  [sweep_blocks(): jnp.einsum('gab,gar->gbr', inverses[:, sweep_step_index], local_side, pre...]
where the time goes in v1:
time: 2020 us; the launch traced here: 2000 us
  waiting for transfers between devices  1610 us (80%)
  local copies, waits for them, and re-layouts  184 us (9%)
  matrix products  91.8 us (5%)
  other arithmetic  88.3 us (4%)
    all_gather x24, waiting for transfers between devices, sweep_blocks(): lax.all_gather(inverse_part, ('prow', 'pcol'))  1560 us
    reduce_sum x24, other arithmetic, sweep_blocks(): jnp.sum(lax.all_gather(inverse_part, ('prow', 'pcol')), axis=0)  84.6 us
    unnamed x37, local copies, waits for them, and re-layouts  54.1 us
    dot_general x24, matrix products, sweep_blocks(): jnp.einsum('gab,gar->gbr', inverses[:, sweep_step_index], local_side, pre...  52.2 us
    dynamic_slice x28, local copies, waits for them, and re-layouts, sweep_blocks(): lax.dynamic_slice_in_dim(solved, owned_start, owned_count, 1)  43.5 us
    psum x1, waiting for transfers between devices, per_device(): contrib = lax.psum(contrib_part, 'leaf')  43 us
    scatter x24, local copies, waits for them, and re-layouts, sweep_blocks(): solved = solved.at[:, sweep_step_index].set(block_value)  41.6 us
  transfers between devices with their start and end apart: 25, of which 25 were waited for; matrix products, arithmetic and copies ran while one was open for 1% of the time, Pallas kernels for 0%

profile of v1, /device:TPU:0, one launch (start us, length us, event | category | flops | bytes accessed | tf_op | source)
XLA Modules:
  0.0 2004.6 jit_solution(5347846197804365636)
XLA Ops:
  18.0 73.5 %all-gather.49.cloned.1.call-done = f32[32,256,256]{2,1,0:T(8,128)} async-done(((f32[2,256,256]{2,1,0:T(8,128)}), f32[32,256,256]{2,1,0:T(8,128)}) %all-gather.49.cloned.1.call-update) | async-done | bytes 8388624 | tf_op jit(solution)/shard_map/all_gather | solution.py:31
  107.0 66.3 %all-gather.51.cloned.1.call-done = f32[32,256,256]{2,1,0:T(8,128)} async-done(((f32[2,256,256]{2,1,0:T(8,128)}), f32[32,256,256]{2,1,0:T(8,128)}) %all-gather.51.cloned.1.call-update) | async-done | bytes 8388624 | tf_op jit(solution)/shard_map/all_gather | solution.py:31
  187.5 70.6 %all-gather.53.cloned.1.call-done = f32[32,256,256]{2,1,0:T(8,128)} async-done(((f32[2,256,256]{2,1,0:T(8,128)}), f32[32,256,256]{2,1,0:T(8,128)}) %all-gather.53.cloned.1.call-update) | async-done | bytes 8388624 | tf_op jit(solution)/shard_map/all_gather | solution.py:31
  272.3 70.6 %all-gather.55.cloned.1.call-done = f32[32,256,256]{2,1,0:T(8,128)} async-done(((f32[2,256,256]{2,1,0:T(8,128)}), f32[32,256,256]{2,1,0:T(8,128)}) %all-gather.55.cloned.1.call-update) | async-done | bytes 8388624 | tf_op jit(solution)/shard_map/all_gather | solution.py:31
  357.6 70.2 %all-gather.57.cloned.1.call-done = f32[32,256,256]{2,1,0:T(8,128)} async-done(((f32[2,256,256]{2,1,0:T(8,128)}), f32[32,256,256]{2,1,0:T(8,128)}) %all-gather.57.cloned.1.call-update) | async-done | bytes 8388624 | tf_op jit(solution)/shard_map/all_gather | solution.py:31
  442.0 70.6 %all-gather.59.cloned.1.call-done = f32[32,256,256]{2,1,0:T(8,128)} async-done(((f32[2,256,256]{2,1,0:T(8,128)}), f32[32,256,256]{2,1,0:T(8,128)}) %all-gather.59.cloned.1.call-update) | async-done | bytes 8388624 | tf_op jit(solution)/shard_map/all_gather | solution.py:31
  526.8 70.6 %all-gather.61.cloned.1.call-done = f32[32,256,256]{2,1,0:T(8,128)} async-done(((f32[2,256,256]{2,1,0:T(8,128)}), f32[32,256,256]{2,1,0:T(8,128)}) %all-gather.61.cloned.1.call-update) | async-done | bytes 8388624 | tf_op jit(solution)/shard_map/all_gather | solution.py:31
  614.5 67.8 %all-gather.63.cloned.1.call-done = f32[32,256,256]{2,1,0:T(8,128)} async-done(((f32[2,256,256]{2,1,0:T(8,128)}), f32[32,256,256]{2,1,0:T(8,128)}) %all-gather.63.cloned.1.call-update) | async-done | bytes 8388624 | tf_op jit(solution)/shard_map/all_gather | solution.py:31
  754.7 56.3 %all-gather.65.cloned.1.call-done = f32[4096,256]{0,1:T(8,128)} async-done(((f32[256,256]{0,1:T(8,128)}), f32[4096,256]{0,1:T(8,128)}) %all-gather.65.cloned.1.call-update) | async-done | bytes 4194320 | tf_op jit(solution)/shard_map/all_gather | solution.py:31
  822.0 55.3 %all-gather.67.cloned.1.call-done = f32[4096,256]{0,1:T(8,128)} async-done(((f32[256,256]{0,1:T(8,128)}), f32[4096,256]{0,1:T(8,128)}) %all-gather.67.cloned.1.call-update) | async-done | bytes 4194320 | tf_op jit(solution)/shard_map/all_gather | solution.py:31
  888.0 56.3 %all-gather.69.cloned.1.call-done = f32[4096,256]{0,1:T(8,128)} async-done(((f32[256,256]{0,1:T(8,128)}), f32[4096,256]{0,1:T(8,128)}) %all-gather.69.cloned.1.call-update) | async-done | bytes 4194320 | tf_op jit(solution)/shard_map/all_gather | solution.py:31
  955.3 56.1 %all-gather.71.cloned.1.call-done = f32[4096,256]{0,1:T(8,128)} async-done(((f32[256,256]{0,1:T(8,128)}), f32[4096,256]{0,1:T(8,128)}) %all-gather.71.cloned.1.call-update) | async-done | bytes 4194320 | tf_op jit(solution)/shard_map/all_gather | solution.py:31
  1021.0 56.3 %all-gather.73.cloned.1.call-done = f32[4096,256]{0,1:T(8,128)} async-done(((f32[256,256]{0,1:T(8,128)}), f32[4096,256]{0,1:T(8,128)}) %all-gather.73.cloned.1.call-update) | async-done | bytes 4194320 | tf_op jit(solution)/shard_map/all_gather | solution.py:31
  1086.7 55.2 %all-gather.75.cloned.1.call-done = f32[4096,256]{0,1:T(8,128)} async-done(((f32[256,256]{0,1:T(8,128)}), f32[4096,256]{0,1:T(8,128)}) %all-gather.75.cloned.1.call-update) | async-done | bytes 4194320 | tf_op jit(solution)/shard_map/all_gather | solution.py:31
  1151.4 55.9 %all-gather.77.cloned.1.call-done = f32[4096,256]{0,1:T(8,128)} async-done(((f32[256,256]{0,1:T(8,128)}), f32[4096,256]{0,1:T(8,128)}) %all-gather.77.cloned.1.call-update) | async-done | bytes 4194320 | tf_op jit(solution)/shard_map/all_gather | solution.py:31
  1218.8 53.8 %all-gather.79.cloned.1.call-done = f32[4096,256]{0,1:T(8,128)} async-done(((f32[256,256]{0,1:T(8,128)}), f32[4096,256]{0,1:T(8,128)}) %all-gather.79.cloned.1.call-update) | async-done | bytes 4194320 | tf_op jit(solution)/shard_map/all_gather | solution.py:31
  1289.1 70.3 %all-gather.81.cloned.1.call-done = f32[32,256,256]{2,1,0:T(8,128)} async-done(((f32[2,256,256]{2,1,0:T(8,128)}), f32[32,256,256]{2,1,0:T(8,128)}) %all-gather.81.cloned.1.call-update) | async-done | bytes 8388624 | tf_op jit(solution)/shard_map/all_gather | solution.py:31
  1381.0 67.0 %all-gather.83.cloned.1.call-done = f32[32,256,256]{2,1,0:T(8,128)} async-done(((f32[2,256,256]{2,1,0:T(8,128)}), f32[32,256,256]{2,1,0:T(8,128)}) %all-gather.83.cloned.1.call-update) | async-done | bytes 8388624 | tf_op jit(solution)/shard_map/all_gather | solution.py:31
  1468.1 70.6 %all-gather.85.cloned.1.call-done = f32[32,256,256]{2,1,0:T(8,128)} async-done(((f32[2,256,256]{2,1,0:T(8,128)}), f32[32,256,256]{2,1,0:T(8,128)}) %all-gather.85.cloned.1.call-update) | async-done | bytes 8388624 | tf_op jit(solution)/shard_map/all_gather | solution.py:31
  1558.7 70.6 %all-gather.87.cloned.1.call-done = f32[32,256,256]{2,1,0:T(8,128)} async-done(((f32[2,256,256]{2,1,0:T(8,128)}), f32[32,256,256]{2,1,0:T(8,128)}) %all-gather.87.cloned.1.call-update) | async-done | bytes 8388624 | tf_op jit(solution)/shard_map/all_gather | solution.py:31
  1649.4 70.6 %all-gather.89.cloned.1.call-done = f32[32,256,256]{2,1,0:T(8,128)} async-done(((f32[2,256,256]{2,1,0:T(8,128)}), f32[32,256,256]{2,1,0:T(8,128)}) %all-gather.89.cloned.1.call-update) | async-done | bytes 8388624 | tf_op jit(solution)/shard_map/all_gather | solution.py:31
  1740.2 70.4 %all-gather.91.cloned.1.call-done = f32[32,256,256]{2,1,0:T(8,128)} async-done(((f32[2,256,256]{2,1,0:T(8,128)}), f32[32,256,256]{2,1,0:T(8,128)}) %all-gather.91.cloned.1.call-update) | async-done | bytes 8388624 | tf_op jit(solution)/shard_map/all_gather | solution.py:31
  1830.7 70.6 %all-gather.93.cloned.1.call-done = f32[32,256,256]{2,1,0:T(8,128)} async-done(((f32[2,256,256]{2,1,0:T(8,128)}), f32[32,256,256]{2,1,0:T(8,128)}) %all-gather.93.cloned.1.call-update) | async-done | bytes 8388624 | tf_op jit(solution)/shard_map/all_gather | solution.py:31
  1920.9 69.2 %all-gather.95.cloned.1.call-done = f32[32,256,256]{2,1,0:T(8,128)} async-done(((f32[2,256,256]{2,1,0:T(8,128)}), f32[32,256,256]{2,1,0:T(8,128)}) %all-gather.95.cloned.1.call-update) | async-done | bytes 8388624 | tf_op jit(solution)/shard_map/all_gather | solution.py:31
  (246 shorter events, 424.9 us)
Async XLA Ops:
  17.9 155.3 %all-gather.51.cloned.1.call-start = ((), (), s32[]{:S(2)}) async-start(), calls=%async_computation.2 | async-start | bytes 8912896 | tf_op jit(solution)/shard_map/all_gather | solution.py:31
  103.6 154.6 %all-gather.53.cloned.1.call-start = ((), (), s32[]{:S(2)}) async-start(), calls=%async_computation.3 | async-start | bytes 8912896 | tf_op jit(solution)/shard_map/all_gather | solution.py:31
  187.5 155.5 %all-gather.55.cloned.1.call-start = ((), (), s32[]{:S(2)}) async-start(), calls=%async_computation.4 | async-start | bytes 8912896 | tf_op jit(solution)/shard_map/all_gather | solution.py:31
  272.3 155.5 %all-gather.57.cloned.1.call-start = ((), (), s32[]{:S(2)}) async-start(), calls=%async_computation.5 | async-start | bytes 8912896 | tf_op jit(solution)/shard_map/all_gather | solution.py:31
  357.1 155.5 %all-gather.59.cloned.1.call-start = ((), (), s32[]{:S(2)}) async-start(), calls=%async_computation.6 | async-start | bytes 8912896 | tf_op jit(solution)/shard_map/all_gather | solution.py:31
  441.9 155.5 %all-gather.61.cloned.1.call-start = ((), (), s32[]{:S(2)}) async-start(), calls=%async_computation.7 | async-start | bytes 8912896 | tf_op jit(solution)/shard_map/all_gather | solution.py:31
  526.8 155.6 %all-gather.63.cloned.1.call-start = ((), (), s32[]{:S(2)}) async-start(), calls=%async_computation.8 | async-start | bytes 8912896 | tf_op jit(solution)/shard_map/all_gather | solution.py:31
  611.7 140.7 %all-reduce.6.cloned.1.call-start = ((), (), s32[]{:S(2)}) async-start(), calls=%async_computation | async-start | bytes 524288 | tf_op jit(solution)/shard_map/psum | solution.py:73
  692.4 118.6 %all-gather.65.cloned.1.call-start = ((), (), s32[]{:S(2)}) async-start(), calls=%async_computation.9 | async-start | bytes 4456448 | tf_op jit(solution)/shard_map/all_gather | solution.py:31
  754.4 122.8 %all-gather.67.cloned.1.call-start = ((), (), s32[]{:S(2)}) async-start(), calls=%async_computation.10 | async-start | bytes 4456448 | tf_op jit(solution)/shard_map/all_gather | solution.py:31
  820.9 123.4 %all-gather.69.cloned.1.call-start = ((), (), s32[]{:S(2)}) async-start(), calls=%async_computation.11 | async-start | bytes 4456448 | tf_op jit(solution)/shard_map/all_gather | solution.py:31
  888.0 123.4 %all-gather.71.cloned.1.call-start = ((), (), s32[]{:S(2)}) async-start(), calls=%async_computation.12 | async-start | bytes 4456448 | tf_op jit(solution)/shard_map/all_gather | solution.py:31
  955.1 122.3 %all-gather.73.cloned.1.call-start = ((), (), s32[]{:S(2)}) async-start(), calls=%async_computation.13 | async-start | bytes 4456448 | tf_op jit(solution)/shard_map/all_gather | solution.py:31
  1021.0 120.9 %all-gather.75.cloned.1.call-start = ((), (), s32[]{:S(2)}) async-start(), calls=%async_computation.14 | async-start | bytes 4456448 | tf_op jit(solution)/shard_map/all_gather | solution.py:31
  1085.5 121.8 %all-gather.77.cloned.1.call-start = ((), (), s32[]{:S(2)}) async-start(), calls=%async_computation.15 | async-start | bytes 4456448 | tf_op jit(solution)/shard_map/all_gather | solution.py:31
  1150.9 121.8 %all-gather.79.cloned.1.call-start = ((), (), s32[]{:S(2)}) async-start(), calls=%async_computation.16 | async-start | bytes 4456448 | tf_op jit(solution)/shard_map/all_gather | solution.py:31
  1216.3 143.1 %all-gather.81.cloned.1.call-start = ((), (), s32[]{:S(2)}) async-start(), calls=%async_computation.17 | async-start | bytes 8912896 | tf_op jit(solution)/shard_map/all_gather | solution.py:31
  1289.1 159.0 %all-gather.83.cloned.1.call-start = ((), (), s32[]{:S(2)}) async-start(), calls=%async_computation.18 | async-start | bytes 8912896 | tf_op jit(solution)/shard_map/all_gather | solution.py:31
  1377.4 161.3 %all-gather.85.cloned.1.call-start = ((), (), s32[]{:S(2)}) async-start(), calls=%async_computation.19 | async-start | bytes 8912896 | tf_op jit(solution)/shard_map/all_gather | solution.py:31
  1468.0 161.3 %all-gather.87.cloned.1.call-start = ((), (), s32[]{:S(2)}) async-start(), calls=%async_computation.20 | async-start | bytes 8912896 | tf_op jit(solution)/shard_map/all_gather | solution.py:31
  1558.7 161.3 %all-gather.89.cloned.1.call-start = ((), (), s32[]{:S(2)}) async-start(), calls=%async_computation.21 | async-start | bytes 8912896 | tf_op jit(solution)/shard_map/all_gather | solution.py:31
  1649.3 161.3 %all-gather.91.cloned.1.call-start = ((), (), s32[]{:S(2)}) async-start(), calls=%async_computation.22 | async-start | bytes 8912896 | tf_op jit(solution)/shard_map/all_gather | solution.py:31
  1740.0 161.3 %all-gather.93.cloned.1.call-start = ((), (), s32[]{:S(2)}) async-start(), calls=%async_computation.23 | async-start | bytes 8912896 | tf_op jit(solution)/shard_map/all_gather | solution.py:31
  1830.6 159.5 %all-gather.95.cloned.1.call-start = ((), (), s32[]{:S(2)}) async-start(), calls=%async_computation.24 | async-start | bytes 8912896 | tf_op jit(solution)/shard_map/all_gather | solution.py:31
  (9 other events, 1491.4 us)
Sparse Core Ops, SparseCore 0:
  18.1 73.4 all-gather.48
  103.7 69.5 all-gather.50
  187.6 70.5 all-gather.52
  272.4 70.5 all-gather.54
  357.2 70.5 all-gather.56
  442.1 70.5 all-gather.58
  526.9 70.4 all-gather.60
  611.8 70.5 all-gather.62
  692.5 59.7 all-reduce.5
  821.0 56.2 all-gather.66
  888.1 56.1 all-gather.68
  955.2 56.1 all-gather.70
  1021.1 56.1 all-gather.72
  1085.6 56.1 all-gather.74
  1151.0 56.2 all-gather.76
  1216.4 56.1 all-gather.78
  1289.2 70.1 all-gather.80
  1377.5 70.4 all-gather.82
  1468.2 70.4 all-gather.84
  1558.8 70.5 all-gather.86
  1649.5 70.5 all-gather.88
  1740.1 70.5 all-gather.90
  1830.7 70.4 all-gather.92
  1919.6 70.4 all-gather.94
  (1 shorter events, 56.0 us)
